TPU v7x, 32 devices: a whole 2x2x4 slice. The times are simulated.
32 devices in a mesh: var: 16 (over z, y, core), smp: 2 (over x).
Axes of the slice: x: 2, y: 2, z: 4, core: 2. Of those that a mesh axis runs over, the one named last changes fastest.
Arguments:
- genotype: bfloat16 [32768, 2048], P('var', 'smp'), may hold values from 0 to 2
- labels: int32 [32768], P('var'), may hold values from 0 to 7, as said below
- probes: bfloat16 [20, 2048], P(None, 'smp'), may hold values from -6 to 6
- phenotype: bfloat16 [2048], P('smp'), may hold values from -6 to 6
Outputs:
- moments: float32 [8, 21, 2, 1024], P(None, None, 'smp', 'var')
Inputs may be any that keep to these rules, and one draw needn't show every extreme that they name: Within each aligned block of 2048 variants the labels never fall, and every one of the 8 components appears in every block.
All inputs are finite; a program needn't handle non-finite values.
Results may differ from a plain program's by a relative error of at most 0.0039.
Values sent between devices are 32-bit elements; how exact they have to be, the bound alone decides.
A program may use at most 64 MiB of HBM per device.

v0:
```python
import jax
import jax.numpy as jnp
from jax import lax
from jax.sharding import PartitionSpec as P

QDEV = 1
K = 8
NV = 21


EPS = 1e-06


def body(genotype, labels, probes, phenotype):
    variants = genotype.shape[0]
    samples = genotype.shape[1]
    total = samples * lax.axis_size("smp")
    member = (labels[None, :] == jnp.arange(K, dtype=jnp.int32)[:, None]).astype(jnp.float32)
    counts = lax.psum(jnp.sum(member, axis=1), "var")
    dosage = genotype.astype(jnp.float32)
    sums = lax.psum(jnp.sum(dosage, axis=1), "smp")
    centered = dosage - (sums / total)[:, None]
    squares = lax.psum(jnp.sum(centered * centered, axis=1), "smp")
    scaled = (centered * lax.rsqrt(squares / total + EPS)[:, None]).astype(jnp.bfloat16)
    vectors = jnp.concatenate([probes, phenotype[None, :]], axis=0)
    partial_value = lax.dot_general(
        vectors, scaled, (((1,), (1,)), ((), ())), preferred_element_type=jnp.float32
    )
    projected = lax.psum(partial_value, "smp")
    weights = (projected[None, :, :] * member[:, None, :] / counts[:, None, None]).astype(
        jnp.bfloat16
    )
    weights = weights.reshape(K * NV, variants)
    terms = jnp.dot(weights, scaled, preferred_element_type=jnp.float32)
    terms = terms.reshape(K, NV, QDEV, samples // QDEV)
    return lax.psum_scatter(terms, "var", scatter_dimension=3, tiled=True)


def solution(mesh):
    placed = (P("var", "smp"), P("var"), P(None, "smp"), P("smp"))
    return jax.shard_map(
        body, mesh=mesh, in_specs=placed, out_specs=P(None, None, "smp", "var"), check_vma=False
    )
```

profile of v0, /device:TPU:0, one launch (start us, length us, event | category | flops | bytes accessed | tf_op | source)
XLA Modules:
  0.0 136.4 jit_solution(874091315711465319)
XLA Ops:
  6.5 0.0 all-reduce.2.cloned.1.call-start
  6.5 0.7 broadcast_in_dim.2
  7.2 2.8 %convert_reduce_fusion = f32[2048]{0:T(1024)S(1)} fusion(bf16[2048,1024]{1,0:T(8,128)(2,1)} %param.4), kind=kLoop, calls=%fused_computation.1 | loop fusion | flops 4192256 | bytes 4202496 | tf_op jit(solution)/shard_map/reduce_sum | solution.py:21
  10.0 5.9 %psum.28 = f32[2048]{0:T(1024)S(1)} all-reduce(f32[2048]{0:T(1024)S(1)} %convert_reduce_fusion), channel_id=1, replica_groups=mesh['var'=16,'smp'=2] {'smp'}, use_global_device_ids=true, to_apply=%region_1.0 | all-reduce | flops 2048 | bytes 16384 | tf_op jit(solution)/shard_map/psum | solution.py:21
  16.0 3.0 %fusion.2 = f32[2048]{0:T(1024)S(1)} fusion(bf16[2048,1024]{1,0:T(8,128)(2,1)} %param.4, f32[2048]{0:T(1024)S(1)} %broadcast_multiply_fusion), kind=kLoop, calls=%fused_computation.4 | loop fusion | flops 8386560 | bytes 4210688 | tf_op jit(solution)/shard_map/reduce_sum | solution.py:23
  19.0 5.0 %psum.29 = f32[2048]{0:T(1024)S(1)} all-reduce(f32[2048]{0:T(1024)S(1)} %fusion.2), channel_id=1, replica_groups=mesh['var'=16,'smp'=2] {'smp'}, use_global_device_ids=true, to_apply=%region_3.0 | all-reduce | flops 2048 | bytes 16384 | tf_op jit(solution)/shard_map/psum | solution.py:23
  24.0 0.0 copy-start.1
  24.0 2.8 %fusion.3 = bf16[2048,1024]{1,0:T(8,128)(2,1)S(1)} fusion(bf16[2048,1024]{1,0:T(8,128)(2,1)} %param.4, f32[2048]{0:T(1024)S(1)} %add_rsqrt_fusion, f32[2048]{0:T(1024)S(1)} %broadcast_multiply_fusion), kind=kLoop, calls=%fused_computation.5 | loop fusion | flops 8388608 | bytes 8404992 | tf_op jit(solution)/shard_map/convert_element_type | solution.py:24
  26.8 0.0 copy-start
  26.8 1.9 %copy-done = bf16[2048,1024]{1,0:T(8,128)(2,1)} copy-done((bf16[2048,1024]{1,0:T(8,128)(2,1)}, bf16[2048,1024]{1,0:T(8,128)(2,1)S(1)}, u32[]{:S(2)}) %copy-start) | copy-done | bytes 4194328
  28.7 0.0 copy-done.1
  28.7 1.9 %fusion.13 = f32[21,2048]{1,0:T(8,128)} fusion(bf16[2048,1024]{1,0:T(8,128)(2,1)S(1)} %fusion.3, bf16[1,1024]{1,0:T(2,128)(2,1)S(1)} %broadcast_in_dim.2, bf16[20,1024]{1,0:T(8,128)(2,1)S(1)} %copy-done.1), kind=kOutput, calls=%fused_computation.15 | convolution fusion | flops 88166400 | bytes 4409344 | tf_op jit(solution)/shard_map/dot_general | solution.py:26
  30.6 0.0 all-reduce.2.cloned.1.call-update
  30.6 0.0 reduce-scatter.4.cloned.1.call-start
  30.7 0.0 copy-done.2
  30.7 0.1 fusion.17
  30.8 31.7 %psum.31 = f32[8]{0:T(128)S(1)} all-reduce(f32[8]{0:T(128)S(1)} %fusion.17), channel_id=1, replica_groups=mesh['var'=16,'smp'=2] {'var'}, use_global_device_ids=true, to_apply=%region_6.0 | all-reduce | flops 8 | bytes 64 | tf_op jit(solution)/shard_map/psum | solution.py:19
  62.5 3.3 %fusion.6 = f32[8,21,1,1024]{3,1,0,2:T(8,128)S(1)} fusion(bf16[2048,1024]{1,0:T(8,128)(2,1)} %copy-done, f32[8]{0:T(128)S(1)} %psum.31, f32[8,2048]{1,0:T(8,128)S(1)} %fusion.12, f32[21,2048]{1,0:T(8,128)} %all-reduce.2.cloned.1.call-done), kind=kOutput, calls=%fused_computation.9 | convolution fusion | flops 705675264 | bytes 5120032 | tf_op jit(solution)/shard_map/dot_general | solution.py:34
  65.9 2.7 %copy.7 = f32[8,21,1,1024]{1,0,2,3:T(8,128)} copy(f32[8,21,1,1024]{3,1,0,2:T(8,128)S(1)} %fusion.6) | data formatting | bytes 1376256
  68.6 4.2 %reshape.41 = f32[1024,168]{1,0:T(8,128)} reshape(f32[1024,1,8,21]{3,2,1,0:T(8,128)} %bitcast.13) | data formatting | bytes 1376256
  72.8 0.0 reduce-scatter.4.cloned.1.call-update
  72.8 55.0 %reduce-scatter.4.cloned.1.call-done = f32[64,168]{1,0:T(8,128)} async-done(((f32[1024,168]{1,0:T(8,128)}), f32[64,168]{1,0:T(8,128)}) %reduce-scatter.4.cloned.1.call-update) | async-done | bytes 43024
  127.8 1.0 reshape.42
  128.8 0.8 copy.6
  (5 shorter events, 0.0 us)
Async XLA Ops:
  6.5 56.0 %all-reduce.2.cloned.1.call-start = ((), (), s32[]{:S(2)}) async-start(), calls=%async_computation.1 | async-start | bytes 393216 | tf_op jit(solution)/shard_map/psum | solution.py:29
  24.0 4.7 %copy-start.1 = (bf16[20,1024]{1,0:T(8,128)(2,1)S(1)}, bf16[20,1024]{1,0:T(8,128)(2,1)}, u32[]{:S(2)}) copy-start(bf16[20,1024]{1,0:T(8,128)(2,1)} %param.6) | copy-start | bytes 122884
  26.8 1.9 %copy-start = (bf16[2048,1024]{1,0:T(8,128)(2,1)}, bf16[2048,1024]{1,0:T(8,128)(2,1)S(1)}, u32[]{:S(2)}) copy-start(bf16[2048,1024]{1,0:T(8,128)(2,1)S(1)} %fusion.3) | copy-start | bytes 12582916
  28.7 2.0 %copy-start.2 = (s32[2048]{0:T(1024)S(1)}, s32[2048]{0:T(1024)}, u32[]{:S(2)}) copy-start(s32[2048]{0:T(1024)} %param.5) | copy-start | bytes 24580
  30.6 97.2 %reduce-scatter.4.cloned.1.call-start = ((), (), s32[]{:S(2)}) async-start(), calls=%async_computation.2 | async-start | bytes 1114112
Sparse Core Ops, SparseCore 0:
  30.8 24.1 all-reduce.1
  72.9 54.8 reduce-scatter.3
where the time goes:
time: 137 us; the launch traced here: 136 us
  waiting for transfers between devices  55 us (40%)
  blocking collectives  42.7 us (31%)
  between operations  13.5 us (10%)
  local copies, waits for them, and re-layouts  11.2 us (8%)
  other arithmetic  8.74 us (6%)
  matrix products  5.22 us (4%)
    unnamed x3, waiting for transfers between devices  55 us
    psum x1, blocking collectives, body(): counts = lax.psum(jnp.sum(member, axis=1), 'var')  31.7 us
    unnamed x9, local copies, waits for them, and re-layouts  9.77 us
    psum x1, blocking collectives, body(): sums = lax.psum(jnp.sum(dosage, axis=1), 'smp')  5.94 us
    psum x1, blocking collectives, body(): squares = lax.psum(jnp.sum(centered * centered, axis=1), 'smp')  5.01 us
    dot_general x1, matrix products, body(): terms = jnp.dot(weights, scaled, preferred_element_type=jnp.float32)  3.34 us
    reduce_sum x1, other arithmetic, body(): squares = lax.psum(jnp.sum(centered * centered, axis=1), 'smp')  2.97 us
    convert_element_type x1, other arithmetic, body(): (centered * lax.rsqrt(squares / total + EPS)[:, None]).astype(jnp.bfloat16)  2.8 us
  transfers between devices with their start and end apart: 2, of which 1 were waited for; matrix products, arithmetic and copies ran while one was open for 0% of the time, Pallas kernels for 0%

commit v1 on v0

v1 whole, which is shorter than its diff:
```python
import functools

import jax
import jax.numpy as jnp
from jax import lax
from jax.experimental import pallas as pl
from jax.experimental.pallas import tpu as pltpu
from jax.sharding import PartitionSpec as P

K = 8
EPS = 1e-06
LANES = 128
CHUNK = 256
MESH = pl.DeviceIdType.MESH


def reverse_bits(value, bits):
    out = 0
    for _ in range(bits):
        out = (out << 1) | (value & 1)
        value >>= 1
    return out


def kernel(nsmp, nvar, g_hbm, lab_ref, probes_ref, phen_ref, out_ref, *scratch):
    levels = (nvar // 2).bit_length() - 1
    tiles = nvar // 2
    (g, vec, psend, precv, vsend, vrecv, w, corr, buf, crecv) = scratch[:10]
    srcs = scratch[10 : 10 + levels]
    keeps = scratch[10 + levels : 10 + 2 * levels]
    recvs = scratch[10 + 2 * levels : 10 + 3 * levels]
    (gsem, p_s, p_r, v_s, v_r, c_s, c_r, h_s, h_r) = scratch[10 + 3 * levels :]
    variants, samples = g.shape
    chunks = variants // CHUNK
    nb = probes_ref.shape[0]
    nv = nb + 1
    prow = psend.shape[1]
    rows = (nv + 1) * K
    half_rows = rows // 2
    total = samples * nsmp

    me_v = lax.axis_index("var")
    me_s = lax.axis_index("smp")
    core = me_v % 2

    def g_copy(i):
        part = pl.ds(i * CHUNK, CHUNK)
        return pltpu.make_async_copy(g_hbm.at[part], g.at[part], gsem.at[i])

    for i in range(chunks):
        g_copy(i).start()

    def smp_peer(o):
        return {"var": me_v, "smp": (me_s + o) % nsmp}

    def var_peer(bit):
        step = 1 << bit
        return {"var": me_v + step - 2 * step * ((me_v // step) % 2), "smp": me_s}

    barrier = pltpu.get_barrier_semaphore()
    for o in range(1, nsmp):
        pl.semaphore_signal(barrier, inc=1, device_id=smp_peer(o), device_id_type=MESH)
    for bit in range(levels + 1):
        pl.semaphore_signal(barrier, inc=1, device_id=var_peer(bit), device_id_type=MESH)

    row = lax.broadcasted_iota(jnp.int32, (vec.shape[0], samples), 0)
    lane = lax.broadcasted_iota(jnp.int32, (vec.shape[0], samples), 1)
    unit = (row == nv) | ((row == nv + 1) & (lane == 0))
    vec[...] = jnp.where(unit, 1.0, 0.0)
    vec[0:nb, :] = probes_ref[...].astype(jnp.float32)
    vec[nb : nb + 1, :] = phen_ref[...].astype(jnp.float32)
    vectors = vec[...].astype(jnp.bfloat16)
    vsum = jnp.sum(vec[0:prow, :], axis=1, keepdims=True)
    vsend[...] = jnp.broadcast_to(vsum, vsend.shape)
    ones = jnp.ones((16, 2 * LANES), jnp.bfloat16)

    def v_copy(o):
        return pltpu.make_async_remote_copy(
            src_ref=vsend, dst_ref=vrecv.at[o - 1], send_sem=v_s.at[o - 1],
            recv_sem=v_r.at[o - 1], device_id=smp_peer(o), device_id_type=MESH,
        )

    def p_copy(o, i):
        return pltpu.make_async_remote_copy(
            src_ref=psend.at[i], dst_ref=precv.at[o - 1, i], send_sem=p_s.at[o - 1, i],
            recv_sem=p_r.at[o - 1, i], device_id=smp_peer(o), device_id_type=MESH,
        )

    nt = (((1,), (1,)), ((), ()))
    for i in range(chunks):
        g_copy(i).wait()
        part = g[i * CHUNK : (i + 1) * CHUNK, :]
        prod = lax.dot_general(vectors, part, nt, preferred_element_type=jnp.float32)
        first = jnp.broadcast_to(part[:, 0:1].astype(jnp.float32), (CHUNK, LANES))
        acc = jnp.zeros((CHUNK, LANES), jnp.float32)
        for t in range(samples // LANES):
            d = part[:, t * LANES : (t + 1) * LANES].astype(jnp.float32) - first
            acc = acc + d * d
        hi = acc.astype(jnp.bfloat16)
        lo = (acc - hi.astype(jnp.float32)).astype(jnp.bfloat16)
        both = jnp.concatenate([hi, lo], axis=1)
        s2 = lax.dot_general(ones, both, nt, preferred_element_type=jnp.float32)[0:1, :]
        psend[i] = prod[0:prow, :]
        shifted = prod[nv : nv + 1, :] - samples * prod[nv + 1 : nv + 2, :]
        m2 = jnp.maximum(s2 - shifted * shifted / samples, 0.0)
        psend[i, nv + 1 : nv + 2, :] = m2
        if i == 0:
            pl.semaphore_wait(barrier, nsmp - 1 + levels + 1)
            for o in range(1, nsmp):
                v_copy(o).start()
        for o in range(1, nsmp):
            p_copy(o, i).start()

    corr[...] = jnp.zeros_like(corr)
    kind = lax.broadcasted_iota(jnp.int32, (K, CHUNK), 0)
    for o in range(1, nsmp):
        v_copy(o).wait()
    vtot = vsend[:, 0:1]
    for o in range(1, nsmp):
        vtot = vtot + vrecv[o - 1][:, 0:1]
    for i in range(chunks):
        cols = pl.ds(i * CHUNK, CHUNK)
        parts = [psend[i]]
        for o in range(1, nsmp):
            p_copy(o, i).wait()
            parts.append(precv[o - 1, i])
        psum = functools.reduce(lambda a, b: a + b, parts)
        mean = psum[nv : nv + 1, :] / total
        m2 = psum[nv + 1 : nv + 2, :]
        for p in parts:
            off = p[nv : nv + 1, :] / samples - mean
            m2 = m2 + samples * off * off
        inv = 1.0 / (m2 / total + EPS)
        a = (psum - mean * vtot) * inv
        member = lab_ref[:, cols] == kind
        mean8 = jnp.broadcast_to(mean, (K, CHUNK))
        for jj in range((nv + 1) // 2):
            pair = []
            for j in (2 * jj, 2 * jj + 1):
                if j < nv:
                    wj = jnp.where(member, jnp.broadcast_to(a[j : j + 1, :], (K, CHUNK)), 0.0)
                    wj = wj.astype(jnp.bfloat16).astype(jnp.float32)
                    cj = wj * mean8
                else:
                    wj = jnp.zeros((K, CHUNK), jnp.float32)
                    cj = jnp.where(member, -1.0, 0.0)
                pair.append(wj)
                fold = functools.reduce(
                    lambda x, y: x + y,
                    [cj[:, t * LANES : (t + 1) * LANES] for t in range(CHUNK // LANES)],
                )
                corr[j * K : (j + 1) * K, :] += fold
            w[2 * K * jj : 2 * K * (jj + 1), cols] = jnp.concatenate(pair, axis=0).astype(jnp.bfloat16)

    def c_copy(p):
        return pltpu.make_async_remote_copy(
            src_ref=buf.at[1 - core, p], dst_ref=crecv.at[p], send_sem=c_s.at[p],
            recv_sem=c_r.at[p], device_id=var_peer(0), device_id_type=MESH,
        )

    shift = jnp.sum(corr[...], axis=1, keepdims=True)
    low_lane = lax.broadcasted_iota(jnp.int32, (half_rows, LANES), 1) < LANES // 2
    weights = w[...]
    for c in range(samples // CHUNK):
        term = jnp.dot(weights, g[:, c * CHUNK : (c + 1) * CHUNK], preferred_element_type=jnp.float32)
        term = term - shift
        for u in range(CHUNK // LANES):
            t = c * (CHUNK // LANES) + u
            p = reverse_bits(t, levels)
            top = term[0:half_rows, u * LANES : (u + 1) * LANES]
            low = term[half_rows:rows, u * LANES : (u + 1) * LANES]
            buf[0, p] = jnp.where(low_lane, top, pltpu.roll(low, LANES // 2, 1))
            buf[1, p] = jnp.where(low_lane, pltpu.roll(top, LANES // 2, 1), low)
            c_copy(p).start()

    for p in range(tiles):
        c_copy(p).wait()
    left, right = buf.at[core], crecv
    count = tiles
    for level in range(levels):
        count //= 2
        bit = (me_v // (2 << level)) % 2
        away = pl.ds((1 - bit) * count, count)
        home = pl.ds(bit * count, count)
        copy = pltpu.make_async_remote_copy(
            src_ref=srcs[level], dst_ref=recvs[level], send_sem=h_s.at[level],
            recv_sem=h_r.at[level], device_id=var_peer(level + 1), device_id_type=MESH,
        )
        srcs[level][...] = left[away] + right[away]
        copy.start()
        keeps[level][...] = left[home] + right[home]
        copy.wait()
        left, right = keeps[level], recvs[level]
    res = left[0] + right[0]
    other = pltpu.roll(res, LANES // 2, 1)
    wide = LANES // 2
    counts = other[half_rows - K : half_rows, 0:wide]
    for j in range(nv):
        src = res if j * K < half_rows else other
        at = j * K % half_rows
        out_ref[:, j, :] = src[at : at + K, 0:wide] / counts


def solution(mesh):
    nvar, nsmp = mesh.shape["var"], mesh.shape["smp"]

    def body(genotype, labels, probes, phenotype):
        variants, samples = genotype.shape
        nv = probes.shape[0] + 1
        tiles = samples // LANES
        levels = tiles.bit_length() - 1
        chunks = variants // CHUNK
        prow = (nv + 2 + 7) // 8 * 8
        rows = (nv + 1) * K
        half = rows // 2
        f32 = jnp.float32
        halves = [pltpu.VMEM((tiles >> (level + 1), half, LANES), f32) for level in range(levels)]
        dma = pltpu.SemaphoreType.DMA
        out = pl.pallas_call(
            functools.partial(kernel, nsmp, nvar),
            out_shape=jax.ShapeDtypeStruct((K, nv, LANES // 2), f32),
            in_specs=[pl.BlockSpec(memory_space=pl.ANY)] + [pl.BlockSpec(memory_space=pltpu.VMEM)] * 3,
            out_specs=pl.BlockSpec(memory_space=pltpu.VMEM),
            scratch_shapes=[
                pltpu.VMEM((variants, samples), jnp.bfloat16),
                pltpu.VMEM((32, samples), f32),
                pltpu.VMEM((chunks, prow, CHUNK), f32),
                pltpu.VMEM((nsmp - 1, chunks, prow, CHUNK), f32),
                pltpu.VMEM((prow, LANES), f32),
                pltpu.VMEM((nsmp - 1, prow, LANES), f32),
                pltpu.VMEM((rows, variants), jnp.bfloat16),
                pltpu.VMEM((rows, LANES), f32),
                pltpu.VMEM((2, tiles, half, LANES), f32),
                pltpu.VMEM((tiles, half, LANES), f32),
                *halves, *halves, *halves,
                dma((chunks,)),
                dma((nsmp - 1, chunks)),
                dma((nsmp - 1, chunks)),
                dma((nsmp - 1,)),
                dma((nsmp - 1,)),
                dma((tiles,)),
                dma((tiles,)),
                dma((levels,)),
                dma((levels,)),
            ],
            compiler_params=pltpu.CompilerParams(
                collective_id=0, has_side_effects=True, vmem_limit_bytes=48 << 20
            ),
        )(genotype, labels.reshape(1, variants), probes, phenotype.reshape(1, samples))
        return out.reshape(K, nv, 1, LANES // 2)

    placed = (P("var", "smp"), P("var"), P(None, "smp"), P("smp"))
    return jax.shard_map(
        body, mesh=mesh, in_specs=placed, out_specs=P(None, None, "smp", "var"), check_vma=False
    )
```

time: 137 us -> 33.8 us (0.25)
  waiting for transfers between devices: 55 us -> 0 us
  blocking collectives: 42.7 us -> 0 us
  Pallas kernels: 0 us -> 28.4 us
  between operations: 13.5 us -> 0.01 us
  other arithmetic: 8.74 us -> 0 us
  local copies, waits for them, and re-layouts: 11.2 us -> 5.09 us
  matrix products: 5.22 us -> 0 us
    unnamed x3 -> x0, waiting for transfers between devices: 55 us -> none
    psum x3 -> x0, blocking collectives: 42.7 us -> none  [the longest x1 31.7 us: body(): counts = lax.psum(jnp.sum(member, axis=1), 'var')]
    pallas_call x0 -> x1, Pallas kernels: none -> 28.4 us  [body(): pl.pallas_call(functools.partial(kernel, nsmp, nvar), out_shape=jax.Shape...]
    unnamed x9 -> x6, local copies, waits for them, and re-layouts: 9.77 us -> 3.68 us
    reduce_sum x3 -> x0, other arithmetic: 5.91 us -> none  [the longest x1 2.97 us: body(): squares = lax.psum(jnp.sum(centered * centered, axis=1), 'smp')]
    dot_general x2 -> x0, matrix products: 5.22 us -> none  [the longest x1 3.34 us: body(): terms = jnp.dot(weights, scaled, preferred_element_type=jnp.float32)]
    convert_element_type x2 -> x0, other arithmetic: 2.81 us -> none  [the longest x1 2.8 us: body(): (centered * lax.rsqrt(squares / total + EPS)[:, None]).astype(jnp.bfloat16)]
    reshape x0 -> x2, local copies, waits for them, and re-layouts: none -> 1.41 us  [the longest x1 0.73 us: body(): return out.reshape(K, nv, 1, LANES // 2)]
  transfers between devices with their start and end apart: 2 -> 0, of which waited for: 1 -> 0; matrix products, arithmetic and copies ran while one was open for 0% -> 0% of each run, Pallas kernels for 0% -> 0%
where the time goes in v1:
time: 33.8 us; the launch traced here: 33.5 us
  Pallas kernels  28.4 us (84%)
  local copies, waits for them, and re-layouts  5.09 us (15%)
    pallas_call x1, Pallas kernels, body(): pl.pallas_call(functools.partial(kernel, nsmp, nvar), out_shape=jax.Shape...  28.4 us
    unnamed x6, local copies, waits for them, and re-layouts  3.68 us
    reshape x1, local copies, waits for them, and re-layouts, body(): return out.reshape(K, nv, 1, LANES // 2)  0.73 us
    reshape x1, local copies, waits for them, and re-layouts, body(): phenotype.reshape(1, samples)  0.69 us

profile of v1, /device:TPU:0, one launch (start us, length us, event | category | flops | bytes accessed | tf_op | source)
XLA Modules:
  0.0 33.5 jit_solution(5107965036230990237)
XLA Ops:
  0.0 0.7 %reshape.10.phen_ref = bf16[1,1024]{1,0:T(2,128)(2,1)S(1)} reshape(bf16[1024]{0:T(1024)(128)(2,1)} %param.7) | data formatting | bytes 4096 | tf_op jit(solution)/shard_map/reshape | solution.py:249
  0.7 0.0 copy-start
  0.7 2.2 %copy-done = bf16[2048,1024]{1,0:T(8,128)(2,1)S(1)} copy-done((bf16[2048,1024]{1,0:T(8,128)(2,1)S(1)}, bf16[2048,1024]{1,0:T(8,128)(2,1)}, u32[]{:S(2)}) %copy-start) | copy-done | bytes 4194328
  2.9 0.0 copy-start.1
  2.9 0.8 %copy-done.1 = bf16[20,1024]{1,0:T(8,128)(2,1)S(1)} copy-done((bf16[20,1024]{1,0:T(8,128)(2,1)S(1)}, bf16[20,1024]{1,0:T(8,128)(2,1)}, u32[]{:S(2)}) %copy-start.1) | copy-done | bytes 40984
  3.7 0.0 copy-start.2
  3.7 0.7 %copy-done.2 = s32[2048]{0:T(1024)S(1)} copy-done((s32[2048]{0:T(1024)S(1)}, s32[2048]{0:T(1024)}, u32[]{:S(2)}) %copy-start.2) | copy-done | bytes 8216
  4.4 28.4 %shard_map.46 = f32[8,21,64]{2,1,0:T(8,128)S(1)} custom-call(bf16[2048,1024]{1,0:T(8,128)(2,1)S(1)} %copy-done, s32[1,2048]{1,0:T(1,128)S(1)} %bitcast.3, bf16[20,1024]{1,0:T(8,128)(2,1)S(1)} %copy-done.1, bf16[1,1024]{1,0:T(2,128)(2,1)S(1)} %reshape.10.phen_ref), custom_call_target="tpu_custom_call" | custom-call | tf_op jit(solution)/shard_map/pallas_call | solution.py:219
  32.8 0.7 %copy.5 = f32[8,21,1,64]{3,2,1,0:T(1,128)} copy(f32[8,21,1,64]{3,1,0,2:T(8,128)S(1)} %bitcast.2) | data formatting | bytes 86016 | tf_op jit(solution)/shard_map/reshape | solution.py:250
Async XLA Ops:
  0.7 2.2 %copy-start = (bf16[2048,1024]{1,0:T(8,128)(2,1)S(1)}, bf16[2048,1024]{1,0:T(8,128)(2,1)}, u32[]{:S(2)}) copy-start(bf16[2048,1024]{1,0:T(8,128)(2,1)} %g_hbm.1) | copy-start | bytes 12582916
  2.9 0.8 %copy-start.1 = (bf16[20,1024]{1,0:T(8,128)(2,1)S(1)}, bf16[20,1024]{1,0:T(8,128)(2,1)}, u32[]{:S(2)}) copy-start(bf16[20,1024]{1,0:T(8,128)(2,1)} %probes_ref.1) | copy-start | bytes 122884
  3.7 0.7 %copy-start.2 = (s32[2048]{0:T(1024)S(1)}, s32[2048]{0:T(1024)}, u32[]{:S(2)}) copy-start(s32[2048]{0:T(1024)} %param.5) | copy-start | bytes 24580

commit v2 on v1

v2 whole, which is shorter than its diff:
```python
import functools

import jax
import jax.numpy as jnp
from jax import lax
from jax.experimental import pallas as pl
from jax.experimental.pallas import tpu as pltpu
from jax.sharding import PartitionSpec as P

K = 8
EPS = 1e-06
LANES = 128
CHUNK = 256
MESH = pl.DeviceIdType.MESH


def kernel(nsmp, nvar, g_hbm, lab_hbm, probes_hbm, phen_hbm, out_ref, *scratch):
    (g, lab_ref, probes_ref, phen_ref, vec, psend, precv, vsend, vrecv, w, corr, acc) = scratch[:12]
    (buf, crecv, ysend, ykeep, yrecv, zsend, zrecv) = scratch[12:19]
    (gsem, i_s, p_s, p_r, v_s, v_r, c_s, c_r, y_s, y_r, z_s, z_r) = scratch[19:]
    variants, samples = g.shape
    chunks = variants // CHUNK
    nz = nvar // 4
    nb = probes_ref.shape[0]
    nv = nb + 1
    prow = psend.shape[1]
    rows = (nv + 1) * K
    half_rows = rows // 2
    total = samples * nsmp

    me_v = lax.axis_index("var")
    me_s = lax.axis_index("smp")
    core = me_v % 2
    why = (me_v // 2) % 2
    zed = me_v // 4

    def g_copy(i):
        part = pl.ds(i * CHUNK, CHUNK)
        return pltpu.make_async_copy(g_hbm.at[part], g.at[part], gsem.at[i])

    small = [
        pltpu.make_async_copy(probes_hbm, probes_ref, i_s.at[0]),
        pltpu.make_async_copy(phen_hbm, phen_ref, i_s.at[1]),
        pltpu.make_async_copy(lab_hbm, lab_ref, i_s.at[2]),
    ]
    for copy in small[:2]:
        copy.start()
    for i in range(chunks):
        g_copy(i).start()
    small[2].start()

    def smp_peer(o):
        return {"var": me_v, "smp": (me_s + o) % nsmp}

    def var_peer(offset):
        at = 0
        for bit in range(nvar.bit_length() - 1):
            step = 1 << bit
            at = at + step * (((me_v // step) + (offset // step)) % 2)
        return {"var": at, "smp": me_s}

    def zed_xor(offset):
        at = 0
        for bit in range(nz.bit_length() - 1):
            step = 1 << bit
            at = at + step * (((zed // step) + (offset // step)) % 2)
        return at

    barrier = pltpu.get_barrier_semaphore()
    for o in range(1, nsmp):
        pl.semaphore_signal(barrier, inc=1, device_id=smp_peer(o), device_id_type=MESH)
    partners = [1, 2] + [4 * o for o in range(1, nz)]
    for offset in partners:
        pl.semaphore_signal(barrier, inc=1, device_id=var_peer(offset), device_id_type=MESH)

    row = lax.broadcasted_iota(jnp.int32, (vec.shape[0], samples), 0)
    lane = lax.broadcasted_iota(jnp.int32, (vec.shape[0], samples), 1)
    unit = (row == nv) | ((row == nv + 1) & (lane == 0))
    vec[...] = jnp.where(unit, 1.0, 0.0)
    small[0].wait()
    small[1].wait()
    vec[0:nb, :] = probes_ref[...].astype(jnp.float32)
    phen = phen_ref[...].astype(jnp.float32)
    for t in range(samples // LANES):
        vec[nb : nb + 1, t * LANES : (t + 1) * LANES] = phen[t : t + 1, :]
    vectors = vec[...].astype(jnp.bfloat16)
    vsum = jnp.sum(vec[0:prow, :], axis=1, keepdims=True)
    vsend[...] = jnp.broadcast_to(vsum, vsend.shape)
    ones = jnp.ones((16, 2 * LANES), jnp.bfloat16)

    def v_copy(o):
        return pltpu.make_async_remote_copy(
            src_ref=vsend, dst_ref=vrecv.at[o - 1], send_sem=v_s.at[o - 1],
            recv_sem=v_r.at[o - 1], device_id=smp_peer(o), device_id_type=MESH,
        )

    def p_copy(o, i):
        return pltpu.make_async_remote_copy(
            src_ref=psend.at[i], dst_ref=precv.at[o - 1, i], send_sem=p_s.at[o - 1, i],
            recv_sem=p_r.at[o - 1, i], device_id=smp_peer(o), device_id_type=MESH,
        )

    nt = (((1,), (1,)), ((), ()))
    for i in range(chunks):
        g_copy(i).wait()
        part = g[i * CHUNK : (i + 1) * CHUNK, :]
        prod = lax.dot_general(vectors, part, nt, preferred_element_type=jnp.float32)
        first = jnp.broadcast_to(part[:, 0:1].astype(jnp.float32), (CHUNK, LANES))
        square = jnp.zeros((CHUNK, LANES), jnp.float32)
        for t in range(samples // LANES):
            d = part[:, t * LANES : (t + 1) * LANES].astype(jnp.float32) - first
            square = square + d * d
        hi = square.astype(jnp.bfloat16)
        lo = (square - hi.astype(jnp.float32)).astype(jnp.bfloat16)
        both = jnp.concatenate([hi, lo], axis=1)
        s2 = lax.dot_general(ones, both, nt, preferred_element_type=jnp.float32)[0:1, :]
        psend[i] = prod[0:prow, :]
        shifted = prod[nv : nv + 1, :] - samples * prod[nv + 1 : nv + 2, :]
        m2 = jnp.maximum(s2 - shifted * shifted / samples, 0.0)
        psend[i, nv + 1 : nv + 2, :] = m2
        if i == 0:
            pl.semaphore_wait(barrier, nsmp - 1 + len(partners))
            for o in range(1, nsmp):
                v_copy(o).start()
        for o in range(1, nsmp):
            p_copy(o, i).start()

    corr[...] = jnp.zeros_like(corr)
    small[2].wait()
    kind = lax.broadcasted_iota(jnp.int32, (K, CHUNK), 0)
    for o in range(1, nsmp):
        v_copy(o).wait()
    vtot = vsend[:, 0:1]
    for o in range(1, nsmp):
        vtot = vtot + vrecv[o - 1][:, 0:1]

    def weigh(i):
        cols = pl.ds(i * CHUNK, CHUNK)
        parts = [psend[i]]
        for o in range(1, nsmp):
            p_copy(o, i).wait()
            parts.append(precv[o - 1, i])
        psum = functools.reduce(lambda a, b: a + b, parts)
        mean = psum[nv : nv + 1, :] / total
        m2 = psum[nv + 1 : nv + 2, :]
        for p in parts:
            off = p[nv : nv + 1, :] / samples - mean
            m2 = m2 + samples * off * off
        inv = 1.0 / (m2 / total + EPS)
        a = (psum - mean * vtot) * inv
        member = lab_ref[:, cols] == kind
        mean8 = jnp.broadcast_to(mean, (K, CHUNK))
        for jj in range((nv + 1) // 2):
            pair = []
            for j in (2 * jj, 2 * jj + 1):
                if j < nv:
                    wj = jnp.where(member, jnp.broadcast_to(a[j : j + 1, :], (K, CHUNK)), 0.0)
                    wj = wj.astype(jnp.bfloat16).astype(jnp.float32)
                    cj = wj * mean8
                else:
                    wj = jnp.zeros((K, CHUNK), jnp.float32)
                    cj = jnp.where(member, -1.0, 0.0)
                pair.append(wj)
                fold = functools.reduce(
                    lambda x, y: x + y,
                    [cj[:, t * LANES : (t + 1) * LANES] for t in range(CHUNK // LANES)],
                )
                corr[j * K : (j + 1) * K, :] += fold
            w[2 * K * jj : 2 * K * (jj + 1), cols] = jnp.concatenate(pair, axis=0).astype(jnp.bfloat16)

    early = chunks * 3 // 4
    for i in range(early):
        weigh(i)
    cut = early * CHUNK
    width = 2 * LANES
    for c in range(nz):
        cols = slice(c * width, (c + 1) * width)
        acc[:, cols] = jnp.dot(w[:, 0:cut], g[0:cut, cols], preferred_element_type=jnp.float32)
    for i in range(early, chunks):
        weigh(i)

    def c_copy(u):
        return pltpu.make_async_remote_copy(
            src_ref=buf.at[1 - core, u], dst_ref=crecv.at[u], send_sem=c_s.at[u],
            recv_sem=c_r.at[u], device_id=var_peer(1), device_id_type=MESH,
        )

    def y_copy(u):
        return pltpu.make_async_remote_copy(
            src_ref=ysend.at[u], dst_ref=yrecv.at[u], send_sem=y_s.at[u],
            recv_sem=y_r.at[u], device_id=var_peer(2), device_id_type=MESH,
        )

    def z_copy(u):
        return pltpu.make_async_remote_copy(
            src_ref=zsend.at[u], dst_ref=zrecv.at[u], send_sem=z_s.at[u],
            recv_sem=z_r.at[u], device_id=var_peer(4 * (nz - 1 - u)), device_id_type=MESH,
        )

    shift = jnp.sum(corr[...], axis=1, keepdims=True)
    low_lane = lax.broadcasted_iota(jnp.int32, (half_rows, LANES), 1) < LANES // 2
    tail = w[:, cut:variants]

    def step_c(u):
        cols = pl.ds(pl.multiple_of(zed_xor(nz - 1 - u) * width, width), width)
        term = acc[:, cols] + jnp.dot(tail, g[cut:variants, cols], preferred_element_type=jnp.float32)
        term = term - shift
        for t in range(2):
            top = term[0:half_rows, t * LANES : (t + 1) * LANES]
            low = term[half_rows:rows, t * LANES : (t + 1) * LANES]
            buf[0, u, t] = jnp.where(low_lane, top, pltpu.roll(low, LANES // 2, 1))
            buf[1, u, t] = jnp.where(low_lane, pltpu.roll(top, LANES // 2, 1), low)
        c_copy(u).start()

    def step_y(u):
        c_copy(u).wait()
        ysend[u] = buf[core, u, 1 - why] + crecv[u, 1 - why]
        y_copy(u).start()
        ykeep[u] = buf[core, u, why] + crecv[u, why]

    def step_z(u):
        y_copy(u).wait()
        zsend[u] = ykeep[u] + yrecv[u]
        if u < nz - 1:
            z_copy(u).start()

    for s in range(nz + 3):
        if s < nz:
            step_c(s)
        if 0 <= s - 1 < nz:
            step_y(s - 1)
        if 0 <= s - 3 < nz:
            step_z(s - 3)

    res = zsend[nz - 1]
    for u in range(nz - 2, -1, -1):
        z_copy(u).wait()
        res = res + zrecv[u]
    other = pltpu.roll(res, LANES // 2, 1)
    wide = LANES // 2
    counts = other[half_rows - K : half_rows, 0:wide]
    for j in range(nv):
        src = res if j * K < half_rows else other
        at = j * K % half_rows
        out_ref[:, j, :] = src[at : at + K, 0:wide] / counts


def solution(mesh):
    nvar, nsmp = mesh.shape["var"], mesh.shape["smp"]

    def body(genotype, labels, probes, phenotype):
        variants, samples = genotype.shape
        nb = probes.shape[0]
        nv = nb + 1
        nz = nvar // 4
        chunks = variants // CHUNK
        prow = (nv + 2 + 7) // 8 * 8
        rows = (nv + 1) * K
        half = rows // 2
        f32 = jnp.float32
        dma = pltpu.SemaphoreType.DMA
        out = pl.pallas_call(
            functools.partial(kernel, nsmp, nvar),
            out_shape=jax.ShapeDtypeStruct((K, nv, LANES // 2), f32),
            in_specs=[pl.BlockSpec(memory_space=pltpu.MemorySpace.HBM)] * 4,
            out_specs=pl.BlockSpec(memory_space=pltpu.VMEM),
            scratch_shapes=[
                pltpu.VMEM((variants, samples), jnp.bfloat16),
                pltpu.VMEM((1, variants), jnp.int32),
                pltpu.VMEM((nb, samples), jnp.bfloat16),
                pltpu.VMEM((samples // LANES, LANES), jnp.bfloat16),
                pltpu.VMEM((32, samples), f32),
                pltpu.VMEM((chunks, prow, CHUNK), f32),
                pltpu.VMEM((nsmp - 1, chunks, prow, CHUNK), f32),
                pltpu.VMEM((prow, LANES), f32),
                pltpu.VMEM((nsmp - 1, prow, LANES), f32),
                pltpu.VMEM((rows, variants), jnp.bfloat16),
                pltpu.VMEM((rows, LANES), f32),
                pltpu.VMEM((rows, samples), f32),
                pltpu.VMEM((2, nz, 2, half, LANES), f32),
                pltpu.VMEM((nz, 2, half, LANES), f32),
                pltpu.VMEM((nz, half, LANES), f32),
                pltpu.VMEM((nz, half, LANES), f32),
                pltpu.VMEM((nz, half, LANES), f32),
                pltpu.VMEM((nz, half, LANES), f32),
                pltpu.VMEM((nz - 1, half, LANES), f32),
                dma((chunks,)),
                dma((3,)),
                dma((nsmp - 1, chunks)),
                dma((nsmp - 1, chunks)),
                dma((nsmp - 1,)),
                dma((nsmp - 1,)),
                dma((nz,)),
                dma((nz,)),
                dma((nz,)),
                dma((nz,)),
                dma((nz - 1,)),
                dma((nz - 1,)),
            ],
            compiler_params=pltpu.CompilerParams(
                collective_id=0, has_side_effects=True, vmem_limit_bytes=67043328
            ),
        )(genotype, labels.reshape(1, variants), probes, phenotype.reshape(samples // LANES, LANES))
        return out.reshape(K, nv, 1, LANES // 2)

    placed = (P("var", "smp"), P("var"), P(None, "smp"), P("smp"))
    return jax.shard_map(
        body, mesh=mesh, in_specs=placed, out_specs=P(None, None, "smp", "var"), check_vma=False
    )
```

time: 33.8 us -> 26.2 us (0.78)
  Pallas kernels: 28.4 us -> 24.4 us
  local copies, waits for them, and re-layouts: 5.09 us -> 1.62 us
    pallas_call x1, Pallas kernels: 28.4 us -> 24.4 us  [body(): pl.pallas_call(functools.partial(kernel, nsmp, nvar), out_shape=jax.Shape...]
    unnamed x6 -> x0, local copies, waits for them, and re-layouts: 3.68 us -> none
    reshape x1, local copies, waits for them, and re-layouts: 0.73 us -> 1.62 us  [body(): return out.reshape(K, nv, 1, LANES // 2)]
    reshape x1 -> x0, local copies, waits for them, and re-layouts: 0.69 us -> none  [body(): phenotype.reshape(1, samples)]
where the time goes in v2:
time: 26.2 us; the launch traced here: 26.1 us
  Pallas kernels  24.4 us (93%)
  local copies, waits for them, and re-layouts  1.62 us (6%)
    pallas_call x1, Pallas kernels, body(): pl.pallas_call(functools.partial(kernel, nsmp, nvar), out_shape=jax.Shape...  24.4 us
    reshape x1, local copies, waits for them, and re-layouts, body(): return out.reshape(K, nv, 1, LANES // 2)  1.62 us

profile of v2, /device:TPU:0, one launch (start us, length us, event | category | flops | bytes accessed | tf_op | source)
XLA Modules:
  0.0 26.1 jit_solution(6665036832892546222)
XLA Ops:
  0.0 24.4 %shard_map.46 = f32[8,21,64]{2,1,0:T(8,128)} custom-call(bf16[2048,1024]{1,0:T(8,128)(2,1)} %g_hbm.1, s32[1,2048]{1,0:T(1,128)} %bitcast.4, bf16[20,1024]{1,0:T(8,128)(2,1)} %probes_hbm.1, bf16[8,128]{1,0:T(8,128)(2,1)} %bitcast.5), custom_call_target="tpu_custom_call" | custom-call | tf_op jit(solution)/shard_map/pallas_call | solution.py:262
  24.4 1.6 %copy.5 = f32[8,21,1,64]{3,2,1,0:T(1,128)} copy(f32[8,21,1,64]{3,1,0,2:T(8,128)} %bitcast.3) | data formatting | bytes 86016 | tf_op jit(solution)/shard_map/reshape | solution.py:304

commit v3 on v2

--- a/solution.py
+++ b/solution.py
@@ -17,7 +17,7 @@
 def kernel(nsmp, nvar, g_hbm, lab_hbm, probes_hbm, phen_hbm, out_ref, *scratch):
     (g, lab_ref, probes_ref, phen_ref, vec, psend, precv, vsend, vrecv, w, corr, acc) = scratch[:12]
     (buf, crecv, ysend, ykeep, yrecv, zsend, zrecv) = scratch[12:19]
-    (gsem, i_s, p_s, p_r, v_s, v_r, c_s, c_r, y_s, y_r, z_s, z_r) = scratch[19:]
+    (gsem, i_s, p_s, p_r, v_s, v_r, c_s, c_r, y_s, y_r, z_s, z_r, word) = scratch[19:]
     variants, samples = g.shape
     chunks = variants // CHUNK
     nz = nvar // 4
@@ -69,9 +69,30 @@
     barrier = pltpu.get_barrier_semaphore()
     for o in range(1, nsmp):
         pl.semaphore_signal(barrier, inc=1, device_id=smp_peer(o), device_id_type=MESH)
-    partners = [1, 2] + [4 * o for o in range(1, nz)]
-    for offset in partners:
+    for offset in (1, 2):
         pl.semaphore_signal(barrier, inc=1, device_id=var_peer(offset), device_id_type=MESH)
+    beside = jnp.where(zed > 0, 1, 0) + jnp.where(zed < nz - 1, 1, 0)
+
+    def tell(sem):
+        @pl.when(zed > 0)
+        def _():
+            pl.semaphore_signal(
+                sem, inc=1, device_id={"var": me_v - 4, "smp": me_s}, device_id_type=MESH
+            )
+
+        @pl.when(zed < nz - 1)
+        def _():
+            pl.semaphore_signal(
+                sem, inc=1, device_id={"var": me_v + 4, "smp": me_s}, device_id_type=MESH
+            )
+
+    def hear(r):
+        if r < nz - 2:
+            pl.semaphore_wait(word.at[r], beside)
+            if r + 1 < nz - 2:
+                tell(word.at[r + 1])
+
+    tell(barrier)
 
     row = lax.broadcasted_iota(jnp.int32, (vec.shape[0], samples), 0)
     lane = lax.broadcasted_iota(jnp.int32, (vec.shape[0], samples), 1)
@@ -119,7 +140,9 @@
         m2 = jnp.maximum(s2 - shifted * shifted / samples, 0.0)
         psend[i, nv + 1 : nv + 2, :] = m2
         if i == 0:
-            pl.semaphore_wait(barrier, nsmp - 1 + len(partners))
+            pl.semaphore_wait(barrier, nsmp - 1 + 2 + beside)
+            if nz > 2:
+                tell(word.at[0])
             for o in range(1, nsmp):
                 v_copy(o).start()
         for o in range(1, nsmp):
@@ -127,6 +150,8 @@
 
     corr[...] = jnp.zeros_like(corr)
     small[2].wait()
+    for r in range(nz - 2):
+        hear(r)
     kind = lax.broadcasted_iota(jnp.int32, (K, CHUNK), 0)
     for o in range(1, nsmp):
         v_copy(o).wait()
@@ -296,11 +321,22 @@
                 dma((nz,)),
                 dma((nz - 1,)),
                 dma((nz - 1,)),
+                pltpu.SemaphoreType.REGULAR((max(nz - 2, 1),)),
             ],
             compiler_params=pltpu.CompilerParams(
-                collective_id=0, has_side_effects=True, vmem_limit_bytes=67043328
+                collective_id=0, has_side_effects=True, vmem_limit_bytes=48 << 20
             ),
-        )(genotype, labels.reshape(1, variants), probes, phenotype.reshape(samples // LANES, LANES))
+        )(
+            *[
+                pltpu.with_memory_space_constraint(x, pltpu.HBM)
+                for x in (
+                    genotype,
+                    labels.reshape(1, variants),
+                    probes,
+                    phenotype.reshape(samples // LANES, LANES),
+                )
+            ]
+        )
         return out.reshape(K, nv, 1, LANES // 2)
 
     placed = (P("var", "smp"), P("var"), P(None, "smp"), P("smp"))

time: 26.2 us -> 24.7 us (0.943)
  local copies, waits for them, and re-layouts: 1.62 us -> 0.73 us
  Pallas kernels: 24.4 us -> 23.9 us
    reshape x1, local copies, waits for them, and re-layouts: 1.62 us -> 0.73 us  [body(): return out.reshape(K, nv, 1, LANES // 2)]
    pallas_call x1, Pallas kernels: 24.4 us -> 23.9 us  [body(): pl.pallas_call(functools.partial(kernel, nsmp, nvar), out_shape=jax.Shape...]
where the time goes in v3:
time: 24.7 us; the launch traced here: 24.6 us
  Pallas kernels  23.9 us (97%)
  local copies, waits for them, and re-layouts  0.73 us (3%)
    pallas_call x1, Pallas kernels, body(): pl.pallas_call(functools.partial(kernel, nsmp, nvar), out_shape=jax.Shape...  23.9 us
    reshape x1, local copies, waits for them, and re-layouts, body(): return out.reshape(K, nv, 1, LANES // 2)  0.73 us

profile of v3, /device:TPU:0, one launch (start us, length us, event | category | flops | bytes accessed | tf_op | source)
XLA Modules:
  0.0 24.6 jit_solution(15642293422164893150)
XLA Ops:
  0.0 23.9 %shard_map.46 = f32[8,21,64]{2,1,0:T(8,128)S(1)} custom-call(bf16[2048,1024]{1,0:T(8,128)(2,1)} %g_hbm.1, s32[1,2048]{1,0:T(1,128)} %bitcast.4, bf16[20,1024]{1,0:T(8,128)(2,1)} %probes_hbm.1, bf16[8,128]{1,0:T(8,128)(2,1)} %bitcast.5), custom_call_target="tpu_custom_call" | custom-call | tf_op jit(solution)/shard_map/pallas_call | solution.py:287
  23.9 0.7 %copy.5 = f32[8,21,1,64]{3,2,1,0:T(1,128)} copy(f32[8,21,1,64]{3,1,0,2:T(8,128)S(1)} %bitcast.3) | data formatting | bytes 86016 | tf_op jit(solution)/shard_map/reshape | solution.py:340

commit v4 on v3

--- a/solution.py
+++ b/solution.py
@@ -10,14 +10,15 @@
 K = 8
 EPS = 1e-06
 LANES = 128
-CHUNK = 256
+CHUNK = 512
+SPLIT = 24
 MESH = pl.DeviceIdType.MESH
 
 
 def kernel(nsmp, nvar, g_hbm, lab_hbm, probes_hbm, phen_hbm, out_ref, *scratch):
     (g, lab_ref, probes_ref, phen_ref, vec, psend, precv, vsend, vrecv, w, corr, acc) = scratch[:12]
-    (buf, crecv, ysend, ykeep, yrecv, zsend, zrecv) = scratch[12:19]
-    (gsem, i_s, p_s, p_r, v_s, v_r, c_s, c_r, y_s, y_r, z_s, z_r, word) = scratch[19:]
+    (buf, crecv, ysend, ykeep, yrecv, zsend, zrecv, asend, arecv, bsend, brecv) = scratch[12:23]
+    (gsem, i_s, p_s, p_r, v_s, v_r, c_s, c_r, y_s, y_r, z_s, z_r, a_s, a_r, b_s, b_r, word) = scratch[23:]
     variants, samples = g.shape
     chunks = variants // CHUNK
     nz = nvar // 4
@@ -193,7 +194,7 @@
                 corr[j * K : (j + 1) * K, :] += fold
             w[2 * K * jj : 2 * K * (jj + 1), cols] = jnp.concatenate(pair, axis=0).astype(jnp.bfloat16)
 
-    early = chunks * 3 // 4
+    early = chunks // 2
     for i in range(early):
         weigh(i)
     cut = early * CHUNK
@@ -221,6 +222,18 @@
             src_ref=zsend.at[u], dst_ref=zrecv.at[u], send_sem=z_s.at[u],
             recv_sem=z_r.at[u], device_id=var_peer(4 * (nz - 1 - u)), device_id_type=MESH,
         )
+
+    def a_copy(u):
+        return pltpu.make_async_remote_copy(
+            src_ref=asend.at[u], dst_ref=arecv.at[u], send_sem=a_s.at[u],
+            recv_sem=a_r.at[u], device_id=var_peer(4 * (nz - 1 - u)), device_id_type=MESH,
+        )
+
+    b_copy = pltpu.make_async_remote_copy(
+        src_ref=bsend.at[1 - why], dst_ref=brecv, send_sem=b_s.at[0],
+        recv_sem=b_r.at[0], device_id=var_peer(2), device_id_type=MESH,
+    )
+    first_rows = half_rows - SPLIT
 
     shift = jnp.sum(corr[...], axis=1, keepdims=True)
     low_lane = lax.broadcasted_iota(jnp.int32, (half_rows, LANES), 1) < LANES // 2
@@ -239,9 +252,13 @@
 
     def step_y(u):
         c_copy(u).wait()
-        ysend[u] = buf[core, u, 1 - why] + crecv[u, 1 - why]
+        upper, lower = pl.ds(0, first_rows), pl.ds(first_rows, SPLIT)
+        ysend[u] = buf[core, u, 1 - why, upper] + crecv[u, 1 - why, upper]
         y_copy(u).start()
-        ykeep[u] = buf[core, u, why] + crecv[u, why]
+        asend[u] = buf[core, u, :, lower] + crecv[u, :, lower]
+        if u < nz - 1:
+            a_copy(u).start()
+        ykeep[u] = buf[core, u, why, upper] + crecv[u, why, upper]
 
     def step_z(u):
         y_copy(u).wait()
@@ -257,10 +274,18 @@
         if 0 <= s - 3 < nz:
             step_z(s - 3)
 
+    part = asend[nz - 1]
+    for u in range(nz - 2, -1, -1):
+        a_copy(u).wait()
+        part = part + arecv[u]
+    bsend[...] = part
+    b_copy.start()
     res = zsend[nz - 1]
     for u in range(nz - 2, -1, -1):
         z_copy(u).wait()
         res = res + zrecv[u]
+    b_copy.wait()
+    res = jnp.concatenate([res, bsend[why] + brecv[...]], axis=0)
     other = pltpu.roll(res, LANES // 2, 1)
     wide = LANES // 2
     counts = other[half_rows - K : half_rows, 0:wide]
@@ -304,11 +329,15 @@
                 pltpu.VMEM((rows, samples), f32),
                 pltpu.VMEM((2, nz, 2, half, LANES), f32),
                 pltpu.VMEM((nz, 2, half, LANES), f32),
-                pltpu.VMEM((nz, half, LANES), f32),
-                pltpu.VMEM((nz, half, LANES), f32),
-                pltpu.VMEM((nz, half, LANES), f32),
-                pltpu.VMEM((nz, half, LANES), f32),
-                pltpu.VMEM((nz - 1, half, LANES), f32),
+                pltpu.VMEM((nz, half - SPLIT, LANES), f32),
+                pltpu.VMEM((nz, half - SPLIT, LANES), f32),
+                pltpu.VMEM((nz, half - SPLIT, LANES), f32),
+                pltpu.VMEM((nz, half - SPLIT, LANES), f32),
+                pltpu.VMEM((nz - 1, half - SPLIT, LANES), f32),
+                pltpu.VMEM((nz, 2, SPLIT, LANES), f32),
+                pltpu.VMEM((nz - 1, 2, SPLIT, LANES), f32),
+                pltpu.VMEM((2, SPLIT, LANES), f32),
+                pltpu.VMEM((SPLIT, LANES), f32),
                 dma((chunks,)),
                 dma((3,)),
                 dma((nsmp - 1, chunks)),
@@ -321,6 +350,10 @@
                 dma((nz,)),
                 dma((nz - 1,)),
                 dma((nz - 1,)),
+                dma((nz - 1,)),
+                dma((nz - 1,)),
+                dma((1,)),
+                dma((1,)),
                 pltpu.SemaphoreType.REGULAR((max(nz - 2, 1),)),
             ],
             compiler_params=pltpu.CompilerParams(

time: 24.7 us -> 23 us (0.931)
  Pallas kernels: 23.9 us -> 22.1 us
    pallas_call x1, Pallas kernels: 23.9 us -> 22.1 us  [body(): pl.pallas_call(functools.partial(kernel, nsmp, nvar), out_shape=jax.Shape...]
where the time goes in v4:
time: 23 us; the launch traced here: 22.8 us
  Pallas kernels  22.1 us (96%)
  local copies, waits for them, and re-layouts  0.73 us (3%)
    pallas_call x1, Pallas kernels, body(): pl.pallas_call(functools.partial(kernel, nsmp, nvar), out_shape=jax.Shape...  22.1 us
    reshape x1, local copies, waits for them, and re-layouts, body(): return out.reshape(K, nv, 1, LANES // 2)  0.73 us

profile of v4, /device:TPU:0, one launch (start us, length us, event | category | flops | bytes accessed | tf_op | source)
XLA Modules:
  0.0 22.8 jit_solution(3518240614663682901)
XLA Ops:
  0.0 22.1 %shard_map.46 = f32[8,21,64]{2,1,0:T(8,128)S(1)} custom-call(bf16[2048,1024]{1,0:T(8,128)(2,1)} %g_hbm.1, s32[1,2048]{1,0:T(1,128)} %bitcast.4, bf16[20,1024]{1,0:T(8,128)(2,1)} %probes_hbm.1, bf16[8,128]{1,0:T(8,128)(2,1)} %bitcast.5), custom_call_target="tpu_custom_call" | custom-call | tf_op jit(solution)/shard_map/pallas_call | solution.py:312
  22.1 0.7 %copy.5 = f32[8,21,1,64]{3,2,1,0:T(1,128)} copy(f32[8,21,1,64]{3,1,0,2:T(8,128)S(1)} %bitcast.3) | data formatting | bytes 86016 | tf_op jit(solution)/shard_map/reshape | solution.py:373
